TPU v7x, 32 devices: a whole 2x2x4 slice. The times are simulated.
32 devices in a mesh: imp: 8 (over z, y), camp: 4 (over x, core).
Axes of the slice: x: 2, y: 2, z: 4, core: 2. Of those that a mesh axis runs over, the one named last changes fastest.
Arguments:
- imp_emb: bfloat16 [16384, 256], P(('imp', 'camp')), may hold values from -512 to 512
- imp_cost: bfloat16 [16384], P(('imp', 'camp')), may hold values from 0.099609375 to 1
- camp_emb: bfloat16 [4096, 256], P(('camp', 'imp')), may hold values from -6 to 6
- prices: bfloat16 [4096], P(('camp', 'imp')), may hold values from -5 to 5
- spend_limits: float32 [4096], P(('camp', 'imp')), may hold values from 3 to 32
- block_lists: int32 [128, 4, 8], P('imp', 'camp'), may hold values from 0 to 7, as said below
- block_counts: int32 [128, 4], P('imp', 'camp'), may hold values from 1 to 8, as said below
Outputs:
- new_prices: float32 [4096], P(('camp', 'imp'))
- row_logz: float32 [16384], P('imp')
Inputs may be any that keep to these rules, and one draw needn't show every extreme that they name: `block_lists`: entries of a list of one tile and owner are distinct block numbers of that owner; slots past the count hold block numbers too, which are ignored. `block_counts`: tile 0 uses all 8 slots of every owner.
All inputs are finite; a program needn't handle non-finite values.
Results may differ from a plain program's by a relative error of at most 0.0003.
Values may be sent and summed in bfloat16 or wider, within the bound.
A program may use at most 64 MiB of HBM per device.

v0:
```python
import jax
import jax.numpy as jnp
from jax import lax
from jax.sharding import PartitionSpec as P

D = 256
BLOCK = 128
SLOTS = 8
GROUP = 4


def merged(array, axis, combine):
    everything = jax.tree.map(lambda part: lax.all_gather(part, axis), array)
    initial = jax.tree.map(lambda part: part[0], everything)

    def step(k, so_far):
        return combine(so_far, jax.tree.map(lambda part: part[k], everything))

    return lax.fori_loop(1, lax.axis_size(axis), step, initial)


def local(imp_emb, imp_cost, camp_emb, prices, spend_limits, block_lists, block_counts):
    scale = 3.0 / jnp.sqrt(jnp.float32(D))
    emb_rows, cost_rows = (
        lax.all_gather(imp_emb, "camp", axis=0, tiled=True),
        lax.all_gather(imp_cost, "camp", axis=0, tiled=True),
    )
    camp_all, price_all = (
        lax.all_gather(camp_emb, "imp", axis=0, tiled=True),
        lax.all_gather(prices, "imp", axis=0, tiled=True),
    )
    own_count = camp_all.shape[0] // BLOCK
    camp_table = camp_all.reshape(own_count, BLOCK, D)
    price_table = price_all.astype(jnp.float32).reshape(own_count, BLOCK)
    lists = block_lists[:, 0, :]
    counts = block_counts[:, 0]
    tiles = lists.shape[0]
    turns = tiles // GROUP
    emb_groups = emb_rows.reshape(turns, GROUP, BLOCK, D)
    cost_groups = cost_rows.astype(jnp.float32).reshape(turns, GROUP, BLOCK)
    list_groups = lists.reshape(turns, GROUP, SLOTS)
    count_groups = counts.reshape(turns, GROUP)

    def scores_of(emb, ids, cnt):
        chosen = camp_table[ids]
        chosen_price = price_table[ids]
        raw = jnp.einsum("gbd,gscd->gbsc", emb, chosen, preferred_element_type=jnp.float32)
        logits = raw * scale - chosen_price[:, None, :, :]
        live = (jnp.arange(SLOTS, dtype=jnp.int32)[None, :] < cnt[:, None])[:, None, :, None]
        return (logits, live)

    def local_both(items):
        emb, ids, cnt = items
        logits, live = scores_of(emb, ids, cnt)
        top_here = jnp.max(jnp.where(live, logits, -jnp.inf), axis=(2, 3))
        expo = jnp.exp(jnp.where(live, logits - top_here[:, :, None, None], -jnp.inf))
        return (top_here, jnp.sum(expo, axis=(2, 3)))

    tops_here, totals_here = lax.map(local_both, (emb_groups, list_groups, count_groups))

    def combine(first, second):
        larger = jnp.maximum(first[0], second[0])
        summed = first[1] * jnp.exp(first[0] - larger) + second[1] * jnp.exp(second[0] - larger)
        return (larger, summed)

    top, total = merged((tops_here, totals_here), "camp", combine)
    row_logz = (top + jnp.log(total)).reshape(tiles * BLOCK)
    block_index = jnp.arange(own_count, dtype=jnp.int32)

    def accumulate(spend, items):
        emb, ids, cnt, cost, top_now, total_now = items
        logits, live = scores_of(emb, ids, cnt)
        expo = jnp.exp(jnp.where(live, logits - top_now[:, :, None, None], -jnp.inf))
        weight = expo / total_now[:, :, None, None]
        contrib = jnp.sum(weight * cost[:, :, None, None], axis=1)
        slot_live = jnp.arange(SLOTS, dtype=jnp.int32)[None, :] < cnt[:, None]
        onehot = ((ids[:, :, None] == block_index[None, None, :]) & slot_live[:, :, None]).astype(
            jnp.float32
        )
        added = jnp.einsum("gso,gsc->oc", onehot, contrib, precision=lax.Precision.HIGHEST)
        return (spend + added, None)

    spend_zero = jnp.zeros((own_count, BLOCK), jnp.float32)
    spend, unused = lax.scan(
        accumulate, spend_zero, (emb_groups, list_groups, count_groups, cost_groups, top, total)
    )
    spend = spend.reshape(own_count * BLOCK)
    width = prices.shape[0]
    whole = lax.psum(spend, "imp")
    mine = lax.dynamic_slice_in_dim(whole, lax.axis_index("imp") * width, width)
    new_prices = prices.astype(jnp.float32) + 2.0 * (mine - spend_limits) / (mine + spend_limits)
    return (new_prices, row_logz)


def solution(mesh):
    return jax.shard_map(
        local,
        mesh=mesh,
        in_specs=(
            P(("imp", "camp"), None),
            P(("imp", "camp")),
            P(("camp", "imp"), None),
            P(("camp", "imp")),
            P(("camp", "imp")),
            P("imp", "camp", None),
            P("imp", "camp"),
        ),
        out_specs=(P(("camp", "imp")), P("imp")),
        check_vma=False,
    )
```

profile of v0, /device:TPU:0, one launch (start us, length us, event | category | flops | bytes accessed | tf_op | source)
XLA Modules:
  0.0 137.3 jit_solution(15288913521605371296)
XLA Ops:
  7.2 0.7 all-gather.6.cloned.1.call-update
  7.9 0.8 copy.12
  8.7 22.5 %all-gather.2 = bf16[8,1,128]{2,1,0:T(2,128)(2,1)S(1)} all-gather(bf16[1,1,128]{2,1,0:T(2,128)(2,1)} %bitcast.128), channel_id=1, replica_groups=mesh['imp'=8,'camp'=4] {'imp'}, dimensions={0}, use_global_device_ids=true | all-gather | bytes 2304 | tf_op jit(solution)/shard_map/all_gather | solution.py:30
  31.7 1.2 reduce.3
  33.0 0.7 reshape.223
  33.7 5.2 %all-gather.3 = bf16[4,1,512]{2,1,0:T(2,128)(2,1)S(1)} all-gather(bf16[1,1,512]{2,1,0:T(2,128)(2,1)S(1)} %reshape.223), channel_id=1, replica_groups=mesh['imp'=8,'camp'=4] {'camp'}, dimensions={0}, use_global_device_ids=true | all-gather | bytes 5120 | tf_op jit(solution)/shard_map/all_gather | solution.py:26
  38.9 31.4 %all_gather.25 = bf16[1024,256]{1,0:T(8,128)(2,1)S(1)} all-gather(bf16[128,256]{1,0:T(8,128)(2,1)} %param.15), channel_id=1, replica_groups=mesh['imp'=8,'camp'=4] {'imp'}, dimensions={0}, use_global_device_ids=true | all-gather | bytes 589824 | tf_op jit(solution)/shard_map/all_gather | solution.py:29
  70.3 16.5 %while.40 = (s32[]{:T(128)}, f32[4,4,128]{2,1,0:T(4,128)S(1)}, f32[4,4,128]{2,1,0:T(4,128)S(1)}, s32[4,4]{1,0:T(4,128)S(1)}, bf16[4,4,128,256]{3,2,1,0:T(8,128)(...) while((s32[]{:T(128)}, f32[4,4,128]{2,1,0:T(4,128)S(1)}, ...), condition=%wide.region_3.4_spmd, body=%wide.region_0.3_spmd.sunk | while | flops 273154176 | bytes 10833529 | solution.py:59
  71.0 0.7 gather_fusion.1
  71.7 1.9 %select_reduce_fusion.2 = (f32[4,128]{1,0:T(4,128)S(1)}, f32[4,128,8,128]{1,3,2,0:T(8,128)S(1)}) fusion(f32[4,8,128]{2,1,0:T(8,128)S(1)} %bitcast.117, pred[4,8]{1,0:T(4,128)(4,1)S(1)} %iota_compare_fusion.5, bf16[4,8,128,256]{3,2,1,0:T(8,128)(2,1)S(1)} %bitcast.116, bf16[4,4,128,256]{3,2,1,0:T(8,128)(2,1)} %get-tuple-element.508, ...), kind=kOutput, calls=%fused_computation.11.clone.1 | convolution fusion | flops 270532096 | bytes 4475424 | tf_op jit(solution)/shard_map/while/body/eval_jaxpr/gbd,gscd->gbsc/dot_general | solution.py:47
  73.6 0.8 exponential_reduce_fusion.2
  75.1 0.7 gather_fusion.1
  75.9 1.9 %select_reduce_fusion.2 = (f32[4,128]{1,0:T(4,128)S(1)}, f32[4,128,8,128]{1,3,2,0:T(8,128)S(1)}) fusion(f32[4,8,128]{2,1,0:T(8,128)S(1)} %bitcast.117, pred[4,8]{1,0:T(4,128)(4,1)S(1)} %iota_compare_fusion.5, bf16[4,8,128,256]{3,2,1,0:T(8,128)(2,1)S(1)} %bitcast.116, bf16[4,4,128,256]{3,2,1,0:T(8,128)(2,1)} %get-tuple-element.508, ...), kind=kOutput, calls=%fused_computation.11.clone.1 | convolution fusion | flops 270532096 | bytes 4475424 | tf_op jit(solution)/shard_map/while/body/eval_jaxpr/gbd,gscd->gbsc/dot_general | solution.py:47
  77.7 0.8 exponential_reduce_fusion.2
  79.2 0.7 gather_fusion.1
  80.0 1.9 %select_reduce_fusion.2 = (f32[4,128]{1,0:T(4,128)S(1)}, f32[4,128,8,128]{1,3,2,0:T(8,128)S(1)}) fusion(f32[4,8,128]{2,1,0:T(8,128)S(1)} %bitcast.117, pred[4,8]{1,0:T(4,128)(4,1)S(1)} %iota_compare_fusion.5, bf16[4,8,128,256]{3,2,1,0:T(8,128)(2,1)S(1)} %bitcast.116, bf16[4,4,128,256]{3,2,1,0:T(8,128)(2,1)} %get-tuple-element.508, ...), kind=kOutput, calls=%fused_computation.11.clone.1 | convolution fusion | flops 270532096 | bytes 4475424 | tf_op jit(solution)/shard_map/while/body/eval_jaxpr/gbd,gscd->gbsc/dot_general | solution.py:47
  81.9 0.8 exponential_reduce_fusion.2
  83.4 0.7 gather_fusion.1
  84.1 1.9 %select_reduce_fusion.2 = (f32[4,128]{1,0:T(4,128)S(1)}, f32[4,128,8,128]{1,3,2,0:T(8,128)S(1)}) fusion(f32[4,8,128]{2,1,0:T(8,128)S(1)} %bitcast.117, pred[4,8]{1,0:T(4,128)(4,1)S(1)} %iota_compare_fusion.5, bf16[4,8,128,256]{3,2,1,0:T(8,128)(2,1)S(1)} %bitcast.116, bf16[4,4,128,256]{3,2,1,0:T(8,128)(2,1)} %get-tuple-element.508, ...), kind=kOutput, calls=%fused_computation.11.clone.1 | convolution fusion | flops 270532096 | bytes 4475424 | tf_op jit(solution)/shard_map/while/body/eval_jaxpr/gbd,gscd->gbsc/dot_general | solution.py:47
  86.0 0.8 exponential_reduce_fusion.2
  86.8 5.2 %all-gather = f32[16,4,128]{2,1,0:T(4,128)S(1)} all-gather(f32[4,4,128]{2,1,0:T(4,128)S(1)} %get-tuple-element.235), channel_id=2, replica_groups=mesh['imp'=8,'camp'=4] {'camp'}, dimensions={0}, use_global_device_ids=true | all-gather | bytes 40960 | tf_op jit(solution)/shard_map/all_gather | solution.py:13
  92.0 5.2 %all-gather.1 = f32[16,4,128]{2,1,0:T(4,128)S(1)} all-gather(f32[4,4,128]{2,1,0:T(4,128)S(1)} %get-tuple-element.236), channel_id=3, replica_groups=mesh['imp'=8,'camp'=4] {'camp'}, dimensions={0}, use_global_device_ids=true | all-gather | bytes 40960 | tf_op jit(solution)/shard_map/all_gather | solution.py:13
  97.3 14.7 %while.42 = (s32[]{:T(128)}, f32[8,128]{1,0:T(8,128)S(1)}, s32[4,4,8]{2,1,0:T(4,128)S(1)}, s32[4,4]{1,0:T(4,128)S(1)}, bf16[4,4,128,256]{3,2,1,0:T(8,128)(2,1)},...) while((s32[]{:T(128)}, f32[8,128]{1,0:T(8,128)S(1)}, ...), condition=%wide.region_8.9_spmd.clone, body=%wide.region_6.8_spmd.clone.sunk | while | flops 272498304 | bytes 6668323 | solution.py:84
  97.5 0.7 gather_fusion.2
  98.8 2.0 %multiply_reduce_fusion.2 = f32[4,8,128]{2,1,0:T(8,128)S(1)} fusion(bf16[4,8,128,256]{3,2,1,0:T(8,128)(2,1)S(1)} %bitcast.115, f32[4,128]{1,0:T(4,128)S(1)} %get-tuple-element.484, f32[4,128]{1,0:T(4,128)S(1)} %get-tuple-element.485, f32[4,128]{1,0:T(4,128)S(1)} %dynamic-slice_bitcast_fusion.8, f32[4,8,128]{2,1,0:T(8,128)S(1)} %bitcast.121, ...), kind=kOutput, calls=%fused_computation.24.clone.1 | convolution fusion | flops 272101376 | bytes 2398752 | tf_op jit(solution)/shard_map/while/body/eval_jaxpr/gbd,gscd->gbsc/dot_general | solution.py:47
  101.1 0.7 gather_fusion.2
  102.5 2.0 %multiply_reduce_fusion.2 = f32[4,8,128]{2,1,0:T(8,128)S(1)} fusion(bf16[4,8,128,256]{3,2,1,0:T(8,128)(2,1)S(1)} %bitcast.115, f32[4,128]{1,0:T(4,128)S(1)} %get-tuple-element.484, f32[4,128]{1,0:T(4,128)S(1)} %get-tuple-element.485, f32[4,128]{1,0:T(4,128)S(1)} %dynamic-slice_bitcast_fusion.8, f32[4,8,128]{2,1,0:T(8,128)S(1)} %bitcast.121, ...), kind=kOutput, calls=%fused_computation.24.clone.1 | convolution fusion | flops 272101376 | bytes 2398752 | tf_op jit(solution)/shard_map/while/body/eval_jaxpr/gbd,gscd->gbsc/dot_general | solution.py:47
  104.8 0.7 gather_fusion.2
  106.2 2.0 %multiply_reduce_fusion.2 = f32[4,8,128]{2,1,0:T(8,128)S(1)} fusion(bf16[4,8,128,256]{3,2,1,0:T(8,128)(2,1)S(1)} %bitcast.115, f32[4,128]{1,0:T(4,128)S(1)} %get-tuple-element.484, f32[4,128]{1,0:T(4,128)S(1)} %get-tuple-element.485, f32[4,128]{1,0:T(4,128)S(1)} %dynamic-slice_bitcast_fusion.8, f32[4,8,128]{2,1,0:T(8,128)S(1)} %bitcast.121, ...), kind=kOutput, calls=%fused_computation.24.clone.1 | convolution fusion | flops 272101376 | bytes 2398752 | tf_op jit(solution)/shard_map/while/body/eval_jaxpr/gbd,gscd->gbsc/dot_general | solution.py:47
  108.5 0.7 gather_fusion.2
  109.9 2.0 %multiply_reduce_fusion.2 = f32[4,8,128]{2,1,0:T(8,128)S(1)} fusion(bf16[4,8,128,256]{3,2,1,0:T(8,128)(2,1)S(1)} %bitcast.115, f32[4,128]{1,0:T(4,128)S(1)} %get-tuple-element.484, f32[4,128]{1,0:T(4,128)S(1)} %get-tuple-element.485, f32[4,128]{1,0:T(4,128)S(1)} %dynamic-slice_bitcast_fusion.8, f32[4,8,128]{2,1,0:T(8,128)S(1)} %bitcast.121, ...), kind=kOutput, calls=%fused_computation.24.clone.1 | convolution fusion | flops 272101376 | bytes 2398752 | tf_op jit(solution)/shard_map/while/body/eval_jaxpr/gbd,gscd->gbsc/dot_general | solution.py:47
  112.1 17.2 %psum.7 = f32[1024]{0:T(1024)S(1)} all-reduce(f32[1024]{0:T(1024)S(1)} %bitcast.125), channel_id=1, replica_groups=mesh['imp'=8,'camp'=4] {'imp'}, use_global_device_ids=true, to_apply=%region_9.10 | all-reduce | flops 1024 | bytes 8192 | tf_op jit(solution)/shard_map/psum | solution.py:89
  (89 shorter events, 9.1 us)
Async XLA Ops:
  7.2 63.1 %all-gather.6.cloned.1.call-start = ((), (), s32[]{:S(2)}) async-start(), calls=%async_computation | async-start | bytes 1310720 | tf_op jit(solution)/shard_map/all_gather | solution.py:25
  97.3 32.6 %copy-start = (bf16[128]{0:T(256)(128)(2,1)S(1)}, bf16[128]{0:T(256)(128)(2,1)}, u32[]{:S(2)}) copy-start(bf16[128]{0:T(256)(128)(2,1)} %param.16) | copy-start | bytes 772
  97.3 32.6 %copy-start.1 = (f32[128]{0:T(128)S(1)}, f32[128]{0:T(128)}, u32[]{:S(2)}) copy-start(f32[128]{0:T(128)} %param.17) | copy-start | bytes 1540
Sparse Core Ops, SparseCore 0:
  9.5 19.4 all-gather.5
where the time goes:
time: 138 us; the launch traced here: 137 us
  blocking collectives  86.6 us (63%)
  matrix products  16 us (12%)
  between operations  14.1 us (10%)
  local copies, waits for them, and re-layouts  13 us (9%)
  other arithmetic  6.35 us (5%)
    all_gather x1, blocking collectives, local(): lax.all_gather(camp_emb, 'imp', axis=0, tiled=True)  31.4 us
    all_gather x1, blocking collectives, local(): lax.all_gather(prices, 'imp', axis=0, tiled=True)  22.5 us
    psum x1, blocking collectives, local(): whole = lax.psum(spend, 'imp')  17.2 us
    dot_general x8, matrix products, scores_of(): jnp.einsum('gbd,gscd->gbsc', emb, chosen, preferred_element_type=jnp.floa...  15.3 us
    all_gather x2, blocking collectives, merged(): everything = jax.tree.map(lambda part: lax.all_gather(part, axis), array)  10.4 us
    gather x8, local copies, waits for them, and re-layouts, scores_of(): chosen = camp_table[ids]  5.48 us
    all_gather x1, blocking collectives, local(): lax.all_gather(imp_cost, 'camp', axis=0, tiled=True)  5.18 us
    gather x8, local copies, waits for them, and re-layouts, scores_of(): chosen_price = price_table[ids]  4.59 us
  transfers between devices with their start and end apart: 1, of which 0 were waited for; matrix products, arithmetic and copies ran while one was open for 2% of the time, Pallas kernels for 0%

commit v1 on v0

v1 whole, which is shorter than its diff:
```python
import functools

import jax
import jax.numpy as jnp
from jax import lax
from jax.experimental import pallas as pl
from jax.experimental.pallas import tpu as pltpu
from jax.sharding import PartitionSpec as P

D = 256
BLOCK = 128
LANES = 128
STORE_LIMIT = 24 << 20
MESH = pl.DeviceIdType.MESH


def flip(index, bits, size):
    if size & (size - 1):
        return lax.rem(index + bits, size)
    out, bit = index, 1
    while bit < size:
        if bits & bit:
            out = out + bit * (1 - 2 * lax.rem(index // bit, 2))
        bit *= 2
    return out


def unflip(index, bits, size):
    if size & (size - 1):
        return lax.rem(index + size - bits, size)
    return flip(index, bits, size)


def kernel(
    sizes, emb_ref, cost_ref, camp_ref, price_ref, limit_ref, list_ref, count_ref,
    new_ref, logz_ref,
    e_buf, cost_buf, c_buf, price_buf, p_wide, x_buf, m_buf, s_buf, live_buf, f_buf,
    stat_send, stat_recv, spend_send, spend_recv,
    local_sem, e_send, e_fwd, e_recv, c_send, c_fwd, c_recv, cost_send, cost_recv,
    price_send, price_recv, stat_ssem, stat_rsem, spend_ssem, spend_rsem,
):
    n_imp, n_camp, n_y, chunk = sizes
    n_z, n_x = n_imp // n_y, n_camp // 2
    n_b = n_imp
    n_t = n_camp * chunk
    stored = x_buf.shape[0] == n_b
    me_i, me_c = lax.axis_index("imp"), lax.axis_index("camp")
    z, y = me_i // n_y, lax.rem(me_i, n_y)
    x, k = me_c // 2, lax.rem(me_c, 2)
    partner = 2 * x + (1 - k)
    scale = 3.0 / jnp.sqrt(jnp.float32(D))

    imp_peers = [
        flip(z, dz, n_z) * n_y + flip(y, dy, n_y)
        for dz in range(n_z) for dy in range(n_y) if dz or dy
    ]
    camp_peers = [partner] + [
        2 * flip(x, dx, n_x) + kk for dx in range(1, n_x) for kk in (k, 1 - k)
    ]

    own_copies = [
        pltpu.make_async_copy(camp_ref, c_buf.at[me_i], local_sem.at[0]),
        pltpu.make_async_copy(price_ref, price_buf.at[me_i], local_sem.at[1]),
        pltpu.make_async_copy(cost_ref, cost_buf.at[me_c], local_sem.at[2]),
        pltpu.make_async_copy(emb_ref, e_buf.at[pl.ds(me_c * chunk, chunk)], local_sem.at[3]),
    ]
    for copy in own_copies:
        copy.start()

    barrier = pltpu.get_barrier_semaphore()
    for peer in imp_peers:
        pl.semaphore_signal(barrier, inc=1, device_id={"imp": peer, "camp": me_c}, device_id_type=MESH)
    for peer in camp_peers:
        pl.semaphore_signal(barrier, inc=1, device_id={"imp": me_i, "camp": peer}, device_id_type=MESH)
    pl.semaphore_wait(barrier, len(imp_peers) + len(camp_peers))

    sends = []

    def send(src, dst, ssem, rsem, imp, camp):
        copy = pltpu.make_async_remote_copy(
            src_ref=src, dst_ref=dst, send_sem=ssem, recv_sem=rsem,
            device_id={"imp": imp, "camp": camp}, device_id_type=MESH,
        )
        copy.start()
        sends.append(copy)

    def arrived(dst, ssem, rsem):
        pltpu.make_async_remote_copy(
            src_ref=dst, dst_ref=dst, send_sem=ssem, recv_sem=rsem,
            device_id={"imp": me_i, "camp": partner}, device_id_type=MESH,
        ).wait_recv()

    for dy in range(1, n_y):
        send(camp_ref, c_buf.at[me_i], c_send.at[dy - 1], c_recv.at[me_i],
             z * n_y + flip(y, dy, n_y), me_c)
    for dz in range(1, n_z):
        send(camp_ref, c_buf.at[me_i], c_send.at[n_y - 1 + dz - 1], c_recv.at[me_i],
             flip(z, dz, n_z) * n_y + y, me_c)
    for t in range(chunk):
        for dx in range(1, n_x):
            send(emb_ref.at[t], e_buf.at[me_c * chunk + t], e_send.at[dx, t],
                 e_recv.at[me_c * chunk + t], me_i, 2 * flip(x, dx, n_x) + k)
        send(emb_ref.at[t], e_buf.at[me_c * chunk + t], e_send.at[0, t],
             e_recv.at[me_c * chunk + t], me_i, partner)
    for n, peer in enumerate(imp_peers):
        send(price_ref, price_buf.at[me_i], price_send.at[n], price_recv.at[me_i], peer, me_c)
    for n, peer in enumerate(camp_peers):
        send(cost_ref, cost_buf.at[me_c], cost_send.at[n], cost_recv.at[me_c], me_i, peer)

    slot = lax.broadcasted_iota(jnp.int32, list_ref.shape, 1)
    named = jnp.where(slot < count_ref[...], list_ref[...], -1)

    def mark(b, carry):
        hit = jnp.max(jnp.where(named == b, 1.0, 0.0), axis=1, keepdims=True)
        live_buf[b] = jnp.broadcast_to(hit, (n_t, LANES))
        return carry

    lax.fori_loop(0, n_b, mark, 0)

    for copy in own_copies:
        copy.wait()

    def widen(b):
        p_wide[b] = jnp.broadcast_to(price_buf[b], (BLOCK, LANES)).T

    def score(b, first, count):
        wide = e_buf[pl.ds(first, count)].reshape(count * BLOCK, D)
        raw = lax.dot_general(
            c_buf[b], wide, (((1,), (1,)), ((), ())), preferred_element_type=jnp.float32
        )
        return raw

    def both(b, first, count):
        raw = score(b, first, count)
        for t in range(count):
            logit = raw[:, t * LANES:(t + 1) * LANES] * scale - p_wide[b]
            top = jnp.max(logit, axis=0, keepdims=True)
            expo = jnp.exp(logit - top)
            m_buf[b, pl.ds(first + t, 1), :] = top
            s_buf[b, pl.ds(first + t, 1), :] = jnp.sum(expo, axis=0, keepdims=True)
            if stored:
                x_buf[b, first + t] = expo

    def near(b):
        def step(h, carry):
            both(b, 2 * x * chunk + h * chunk, chunk)
            return carry

        lax.fori_loop(0, 2, step, 0)

    def block_in(b):
        arrived(price_buf.at[b], price_send.at[0], price_recv.at[b])
        widen(b)

    def rows_in(dx, t):
        other = flip(x, dx, n_x)
        tile = (2 * other + k) * chunk + t
        arrived(e_buf.at[tile], e_send.at[0, 0], e_recv.at[tile])
        send(e_buf.at[tile], e_buf.at[tile], e_fwd.at[dx, t], e_recv.at[tile], me_i, partner)

    widen(me_i)
    for t in range(chunk):
        tile = partner * chunk + t
        arrived(e_buf.at[tile], e_send.at[0, 0], e_recv.at[tile])
    near(me_i)

    order = [(0, dy) for dy in range(1, n_y)] + [(dz, 0) for dz in range(1, n_z)]
    order += [(dz, dy) for dz in range(1, n_z) for dy in range(1, n_y)]
    chunks = [(dx, t) for t in range(chunk) for dx in range(1, n_x)]
    for n, (dz, dy) in enumerate(order):
        b = flip(z, dz, n_z) * n_y + flip(y, dy, n_y)
        arrived(c_buf.at[b], c_send.at[0], c_recv.at[b])
        if dy == 0:
            for fy in range(1, n_y):
                send(c_buf.at[b], c_buf.at[b], c_fwd.at[dz, fy], c_recv.at[b],
                     z * n_y + flip(y, fy, n_y), me_c)
        block_in(b)
        near(b)
        if chunks and n < len(order) - 1:
            rows_in(*chunks.pop(0))
    while chunks:
        rows_in(*chunks.pop(0))

    for dx in range(1, n_x):
        other = flip(x, dx, n_x)
        for t in range(chunk):
            tile = (2 * other + (1 - k)) * chunk + t
            arrived(e_buf.at[tile], e_send.at[0, 0], e_recv.at[tile])
        for kk in (k, 1 - k):
            def far(b, carry):
                both(b, (2 * other + kk) * chunk, chunk)
                return carry

            lax.fori_loop(0, n_b, far, 0)

    def block_top(b):
        return jnp.where(live_buf[b] > 0.0, m_buf[b], -jnp.inf)

    top_here = lax.fori_loop(
        0, n_b, lambda b, top: jnp.maximum(top, block_top(b)),
        jnp.full((n_t, LANES), -jnp.inf, jnp.float32),
    )
    total_here = lax.fori_loop(
        0, n_b, lambda b, total: total + s_buf[b] * jnp.exp(block_top(b) - top_here),
        jnp.zeros((n_t, LANES), jnp.float32),
    )
    stat_send[0] = top_here
    stat_send[1] = total_here
    for n, peer in enumerate(camp_peers):
        send(stat_send, stat_recv.at[me_c], stat_ssem.at[n], stat_rsem.at[me_c], me_i, peer)
    for peer in camp_peers:
        arrived(cost_buf.at[peer], cost_send.at[0], cost_recv.at[peer])
    cost = jnp.concatenate([cost_buf[g] for g in range(n_camp)], axis=0)
    stat_recv[me_c] = stat_send[...]
    for peer in camp_peers:
        arrived(stat_recv.at[peer], stat_ssem.at[0], stat_rsem.at[peer])
    top = stat_recv[0, 0]
    for g in range(1, n_camp):
        top = jnp.maximum(top, stat_recv[g, 0])
    total = jnp.zeros_like(top)
    for g in range(n_camp):
        total = total + stat_recv[g, 1] * jnp.exp(stat_recv[g, 0] - top)
    logz_ref[...] = top + jnp.log(total)
    ratio = cost / total

    def factor(b, carry):
        f_buf[b] = ratio * jnp.exp(block_top(b) - top)
        return carry

    lax.fori_loop(0, n_b, factor, 0)

    def spend_of(b):
        def step(h, acc):
            first = h * chunk
            if not stored:
                raw = score(b, first, chunk)
            for t in range(chunk):
                if stored:
                    expo = x_buf[b, first + t]
                else:
                    logit = raw[:, t * LANES:(t + 1) * LANES] * scale - p_wide[b]
                    expo = jnp.exp(logit - m_buf[b, pl.ds(first + t, 1), :])
                acc = acc + expo * f_buf[b, pl.ds(first + t, 1), :]
            return acc

        acc = lax.fori_loop(0, n_camp, step, jnp.zeros((BLOCK, LANES), jnp.float32))
        return jnp.sum(acc.T, axis=0, keepdims=True)

    for n, peer in enumerate(reversed(imp_peers)):
        spend_send[peer] = spend_of(peer)
        send(spend_send.at[peer], spend_recv.at[me_i], spend_ssem.at[n], spend_rsem.at[me_i],
             peer, me_c)
    mine = spend_of(me_i)
    for peer in imp_peers:
        arrived(spend_recv.at[peer], spend_ssem.at[0], spend_rsem.at[peer])
        mine = mine + spend_recv[peer]
    limit = limit_ref[...]
    new_ref[...] = price_buf[me_i] + 2.0 * (mine - limit) / (mine + limit)
    for copy in sends:
        copy.wait_send()


def local(n_y, imp_emb, imp_cost, camp_emb, prices, spend_limits, block_lists, block_counts):
    n_imp, n_camp = lax.axis_size("imp"), lax.axis_size("camp")
    chunk = imp_emb.shape[0] // BLOCK
    n_t = n_camp * chunk
    n_b = n_imp
    n_z = n_imp // n_y
    n_x = n_camp // 2
    f32, bf16 = jnp.float32, jnp.bfloat16
    stored = n_b * n_t * BLOCK * LANES * 4 <= STORE_LIMIT
    dma = pltpu.SemaphoreType.DMA
    anywhere, vmem = pl.BlockSpec(memory_space=pl.ANY), pl.BlockSpec(memory_space=pltpu.VMEM)
    new_prices, logz = pl.pallas_call(
        functools.partial(kernel, (n_imp, n_camp, n_y, chunk)),
        out_shape=(
            jax.ShapeDtypeStruct((1, LANES), f32),
            jax.ShapeDtypeStruct((n_t, LANES), f32),
        ),
        in_specs=[anywhere, anywhere, anywhere, anywhere, vmem, vmem, vmem],
        out_specs=(vmem, vmem),
        scratch_shapes=[
            pltpu.VMEM((n_t, BLOCK, D), bf16),
            pltpu.VMEM((n_camp, chunk, LANES), f32),
            pltpu.VMEM((n_b, BLOCK, D), bf16),
            pltpu.VMEM((n_b, 1, LANES), f32),
            pltpu.VMEM((n_b, BLOCK, LANES), f32),
            pltpu.VMEM((n_b, n_t, BLOCK, LANES) if stored else (1, 1, 8, LANES), f32),
            pltpu.VMEM((n_b, n_t, LANES), f32),
            pltpu.VMEM((n_b, n_t, LANES), f32),
            pltpu.VMEM((n_b, n_t, LANES), f32),
            pltpu.VMEM((n_b, n_t, LANES), f32),
            pltpu.VMEM((2, n_t, LANES), f32),
            pltpu.VMEM((n_camp, 2, n_t, LANES), f32),
            pltpu.VMEM((n_b, 1, LANES), f32),
            pltpu.VMEM((n_b, 1, LANES), f32),
            dma((4,)),
            dma((n_x, chunk)),
            dma((n_x, chunk)),
            dma((n_t,)),
            dma((n_y + n_z,)),
            dma((n_z, n_y)),
            dma((n_b,)),
            dma((n_camp,)),
            dma((n_camp,)),
            dma((n_imp,)),
            dma((n_imp,)),
            dma((n_camp,)),
            dma((n_camp,)),
            dma((n_imp,)),
            dma((n_imp,)),
        ],
        compiler_params=pltpu.CompilerParams(
            collective_id=0, has_side_effects=True, vmem_limit_bytes=60 << 20
        ),
    )(
        imp_emb.reshape(chunk, BLOCK, D),
        imp_cost.astype(f32).reshape(chunk, LANES),
        camp_emb,
        prices.astype(f32).reshape(1, LANES),
        spend_limits.reshape(1, LANES),
        block_lists.reshape(n_t, -1),
        block_counts,
    )
    return new_prices.reshape(-1), logz.reshape(-1)


def rows_of_chips(mesh):
    n_imp = mesh.shape["imp"]
    coords = [getattr(device, "coords", None) for device in mesh.devices[:, 0]]
    if any(place is None for place in coords):
        return 2 if n_imp % 2 == 0 else 1
    return len({place[1] for place in coords})


def solution(mesh):
    return jax.shard_map(
        functools.partial(local, rows_of_chips(mesh)),
        mesh=mesh,
        in_specs=(
            P(("imp", "camp"), None),
            P(("imp", "camp")),
            P(("camp", "imp"), None),
            P(("camp", "imp")),
            P(("camp", "imp")),
            P("imp", "camp", None),
            P("imp", "camp"),
        ),
        out_specs=(P(("camp", "imp")), P("imp")),
        check_vma=False,
    )
```

time: 138 us -> 38.6 us (0.28)
  blocking collectives: 86.6 us -> 0 us
  Pallas kernels: 0 us -> 32.6 us
  matrix products: 16 us -> 0 us
  between operations: 14.1 us -> 0.67 us
  local copies, waits for them, and re-layouts: 13 us -> 3.94 us
  other arithmetic: 6.35 us -> 1.1 us
    all_gather x5 -> x0, blocking collectives: 69.4 us -> none  [the longest x1 31.4 us: local(): lax.all_gather(camp_emb, 'imp', axis=0, tiled=True)]
    pallas_call x0 -> x1, Pallas kernels: none -> 32.6 us  [local(): pl.pallas_call(functools.partial(kernel, (n_imp, n_camp, n_y, chunk)), ou...]
    psum x1 -> x0, blocking collectives: 17.2 us -> none  [local(): whole = lax.psum(spend, 'imp')]
    dot_general x12 -> x0, matrix products: 16 us -> none  [the longest x8 15.3 us: scores_of(): jnp.einsum('gbd,gscd->gbsc', emb, chosen, preferred_element_type=jnp.floa...]
    gather x16 -> x0, local copies, waits for them, and re-layouts: 10.1 us -> none  [the longest x8 5.48 us: scores_of(): chosen = camp_table[ids]]
    reduce_sum x4 -> x0, other arithmetic: 3.11 us -> none  [local_both(): return (top_here, jnp.sum(expo, axis=(2, 3)))]
    unnamed x7 -> x13, local copies, waits for them, and re-layouts: 1.97 us -> 3.28 us
  transfers between devices with their start and end apart: 1 -> 0, of which waited for: 0 -> 0; matrix products, arithmetic and copies ran while one was open for 2% -> 0% of each run, Pallas kernels for 0% -> 0%
where the time goes in v1:
time: 38.6 us; the launch traced here: 38.3 us
  Pallas kernels  32.6 us (84%)
  local copies, waits for them, and re-layouts  3.94 us (10%)
  other arithmetic  1.1 us (3%)
  between operations  0.67 us (2%)
    pallas_call x1, Pallas kernels, local(): pl.pallas_call(functools.partial(kernel, (n_imp, n_camp, n_y, chunk)), ou...  32.6 us
    unnamed x13, local copies, waits for them, and re-layouts  3.28 us

profile of v1, /device:TPU:0, one launch (start us, length us, event | category | flops | bytes accessed | tf_op | source)
XLA Modules:
  0.0 38.3 jit_solution(567376485589457592)
XLA Ops:
  0.6 0.0 copy-start.4
  0.6 0.0 copy-start.1
  0.7 0.6 %copy-done.4 = bf16[128]{0:T(256)(128)(2,1)S(1)} copy-done((bf16[128]{0:T(256)(128)(2,1)S(1)}, bf16[128]{0:T(256)(128)(2,1)}, u32[]{:S(2)}) %copy-start.4) | copy-done | bytes 280
  1.3 0.0 copy-start.2
  1.3 0.5 %bitcast_convert_fusion.1.price_ref = f32[1,128]{1,0:T(1,128)} fusion(bf16[128]{0:T(256)(128)(2,1)S(1)} %copy-done.4), kind=kLoop, calls=%fused_computation.1 | loop fusion | flops 128 | bytes 768 | tf_op jit(solution)/shard_map/reshape | solution.py:320
  1.8 0.2 copy-done.2
  2.0 0.6 %bitcast_convert_fusion.cost_ref = f32[4,128]{1,0:T(4,128)} fusion(bf16[512]{0:T(512)(128)(2,1)S(1)} %copy-done.2), kind=kLoop, calls=%fused_computation | loop fusion | flops 512 | bytes 3072 | tf_op jit(solution)/shard_map/reshape | solution.py:318
  2.6 0.0 copy-done.1
  2.6 0.0 copy-start.3
  2.6 0.7 %copy.9.list_ref = s32[16,8]{1,0:T(8,128)} copy(s32[16,8]{0,1:T(8,128)S(1)} %bitcast.13) | data formatting | bytes 1024 | tf_op jit(solution)/shard_map/reshape | solution.py:322
  3.2 0.0 copy-done.3
  3.2 0.7 %copy.10.count_ref = s32[16,1]{1,0:T(8,128)} copy(s32[16,1]{0,1:T(1,128)S(1)} %copy-done.3) | data formatting | bytes 128 | tf_op args[6]
  3.9 32.6 %shard_map.86 = (f32[1,128]{1,0:T(1,128)}, f32[16,128]{1,0:T(8,128)}) custom-call(bf16[4,128,256]{2,1,0:T(8,128)(2,1)} %bitcast.11, f32[4,128]{1,0:T(4,128)} %bitcast_convert_fusion.cost_ref, bf16[128,256]{1,0:T(8,128)(2,1)} %camp_ref.1, f32[1,128]{1,0:T(1,128)} %bitcast_convert_fusion.1.price_ref, f32[1,128]{1,0:T(1,128)} %bitcast.14, ...), custom_call_target="tpu_custom_call" | custom-call | tf_op jit(solution)/shard_map/pallas_call | solution.py:274
  36.5 0.0 copy-start
  36.5 1.2 %copy.13 = f32[128]{0:T(128)} copy(f32[128]{0:T(128)} %bitcast.15) | data formatting | bytes 1024
  37.7 0.0 copy-done
  37.7 0.6 %copy.14 = f32[2048]{0:T(1024)} copy(f32[2048]{0:T(1024)S(1)} %bitcast.12) | data formatting | bytes 16384
Async XLA Ops:
  0.6 0.7 %copy-start.4 = (bf16[128]{0:T(256)(128)(2,1)S(1)}, bf16[128]{0:T(256)(128)(2,1)}, u32[]{:S(2)}) copy-start(bf16[128]{0:T(256)(128)(2,1)} %param.10) | copy-start | bytes 772
  0.6 1.9 %copy-start.1 = (s32[16,1,8]{0,2,1:T(8,128)S(1)}, s32[16,1,8]{0,2,1:T(8,128)}, u32[]{:S(2)}) copy-start(s32[16,1,8]{0,2,1:T(8,128)} %param.12) | copy-start | bytes 1540
  1.3 0.7 %copy-start.2 = (bf16[512]{0:T(512)(128)(2,1)S(1)}, bf16[512]{0:T(512)(128)(2,1)}, u32[]{:S(2)}) copy-start(bf16[512]{0:T(512)(128)(2,1)} %param.8) | copy-start | bytes 3076
  2.6 0.7 %copy-start.3 = (s32[16,1]{0,1:T(1,128)S(1)}, s32[16,1]{0,1:T(1,128)}, u32[]{:S(2)}) copy-start(s32[16,1]{0,1:T(1,128)} %param.13) | copy-start | bytes 196
  36.5 1.2 %copy-start = (f32[16,128]{1,0:T(8,128)S(1)}, f32[16,128]{1,0:T(8,128)}, u32[]{:S(2)}) copy-start(f32[16,128]{1,0:T(8,128)} %get-tuple-element.5) | copy-start | bytes 24580

commit v2 on v1

--- a/solution.py
+++ b/solution.py
@@ -35,7 +35,8 @@
     sizes, emb_ref, cost_ref, camp_ref, price_ref, limit_ref, list_ref, count_ref,
     new_ref, logz_ref,
     e_buf, cost_buf, c_buf, price_buf, p_wide, x_buf, m_buf, s_buf, live_buf, f_buf,
-    stat_send, stat_recv, spend_send, spend_recv,
+    stat_send, stat_recv, spend_send, spend_recv, cost_raw, price_raw, turn_buf, list_buf,
+    count_buf, limit_buf,
     local_sem, e_send, e_fwd, e_recv, c_send, c_fwd, c_recv, cost_send, cost_recv,
     price_send, price_recv, stat_ssem, stat_rsem, spend_ssem, spend_rsem,
 ):
@@ -60,10 +61,17 @@
 
     own_copies = [
         pltpu.make_async_copy(camp_ref, c_buf.at[me_i], local_sem.at[0]),
-        pltpu.make_async_copy(price_ref, price_buf.at[me_i], local_sem.at[1]),
-        pltpu.make_async_copy(cost_ref, cost_buf.at[me_c], local_sem.at[2]),
-        pltpu.make_async_copy(emb_ref, e_buf.at[pl.ds(me_c * chunk, chunk)], local_sem.at[3]),
+        pltpu.make_async_copy(emb_ref, e_buf.at[pl.ds(me_c * chunk, chunk)], local_sem.at[1]),
     ]
+    small_copies = [
+        pltpu.make_async_copy(price_ref, price_raw, local_sem.at[2]),
+        pltpu.make_async_copy(cost_ref, cost_raw, local_sem.at[3]),
+        pltpu.make_async_copy(list_ref, list_buf, local_sem.at[4]),
+        pltpu.make_async_copy(count_ref, count_buf, local_sem.at[5]),
+        pltpu.make_async_copy(limit_ref, limit_buf, local_sem.at[6]),
+    ]
+    for copy in small_copies:
+        copy.start()
     for copy in own_copies:
         copy.start()
 
@@ -72,6 +80,22 @@
         pl.semaphore_signal(barrier, inc=1, device_id={"imp": peer, "camp": me_c}, device_id_type=MESH)
     for peer in camp_peers:
         pl.semaphore_signal(barrier, inc=1, device_id={"imp": me_i, "camp": peer}, device_id_type=MESH)
+
+    turn_buf[...] = jnp.full(turn_buf.shape, -1, jnp.int32)
+    for copy in small_copies:
+        copy.wait()
+    slot = lax.broadcasted_iota(jnp.int32, list_buf.shape, 0)
+    turn_buf[: list_buf.shape[0], :n_t] = jnp.where(slot < count_buf[...], list_buf[...], -1)
+    named = turn_buf[...].T[:n_t]
+
+    def mark(b, carry):
+        hit = jnp.max(jnp.where(named == b, 1.0, 0.0), axis=1, keepdims=True)
+        live_buf[b] = jnp.broadcast_to(hit, (n_t, LANES))
+        return carry
+
+    lax.fori_loop(0, n_b, mark, 0)
+    price_buf[me_i] = price_raw[...].astype(jnp.float32).reshape(1, LANES)
+    cost_buf[me_c] = cost_raw[...].astype(jnp.float32).reshape(chunk, LANES)
     pl.semaphore_wait(barrier, len(imp_peers) + len(camp_peers))
 
     sends = []
@@ -103,19 +127,9 @@
         send(emb_ref.at[t], e_buf.at[me_c * chunk + t], e_send.at[0, t],
              e_recv.at[me_c * chunk + t], me_i, partner)
     for n, peer in enumerate(imp_peers):
-        send(price_ref, price_buf.at[me_i], price_send.at[n], price_recv.at[me_i], peer, me_c)
+        send(price_buf.at[me_i], price_buf.at[me_i], price_send.at[n], price_recv.at[me_i], peer, me_c)
     for n, peer in enumerate(camp_peers):
-        send(cost_ref, cost_buf.at[me_c], cost_send.at[n], cost_recv.at[me_c], me_i, peer)
-
-    slot = lax.broadcasted_iota(jnp.int32, list_ref.shape, 1)
-    named = jnp.where(slot < count_ref[...], list_ref[...], -1)
-
-    def mark(b, carry):
-        hit = jnp.max(jnp.where(named == b, 1.0, 0.0), axis=1, keepdims=True)
-        live_buf[b] = jnp.broadcast_to(hit, (n_t, LANES))
-        return carry
-
-    lax.fori_loop(0, n_b, mark, 0)
+        send(cost_buf.at[me_c], cost_buf.at[me_c], cost_send.at[n], cost_recv.at[me_c], me_i, peer)
 
     for copy in own_copies:
         copy.wait()
@@ -158,15 +172,20 @@
         arrived(e_buf.at[tile], e_send.at[0, 0], e_recv.at[tile])
         send(e_buf.at[tile], e_buf.at[tile], e_fwd.at[dx, t], e_recv.at[tile], me_i, partner)
 
+    def rows_there(g):
+        for t in range(chunk):
+            tile = g * chunk + t
+            arrived(e_buf.at[tile], e_send.at[0, 0], e_recv.at[tile])
+
     widen(me_i)
-    for t in range(chunk):
-        tile = partner * chunk + t
-        arrived(e_buf.at[tile], e_send.at[0, 0], e_recv.at[tile])
+    rows_there(partner)
     near(me_i)
 
     order = [(0, dy) for dy in range(1, n_y)] + [(dz, 0) for dz in range(1, n_z)]
     order += [(dz, dy) for dz in range(1, n_z) for dy in range(1, n_y)]
     chunks = [(dx, t) for t in range(chunk) for dx in range(1, n_x)]
+    small = n_b * (n_x - 1) <= 8
+    seen, groups = [me_i], []
     for n, (dz, dy) in enumerate(order):
         b = flip(z, dz, n_z) * n_y + flip(y, dy, n_y)
         arrived(c_buf.at[b], c_send.at[0], c_recv.at[b])
@@ -176,19 +195,33 @@
                      z * n_y + flip(y, fy, n_y), me_c)
         block_in(b)
         near(b)
+        for g in groups:
+            both(b, g * chunk, chunk)
+        seen.append(b)
         if chunks and n < len(order) - 1:
             rows_in(*chunks.pop(0))
+        if small and not chunks and len(groups) < 2 * (n_x - 1) and n < len(order) - 1:
+            dx, own = 1 + len(groups) // 2, len(groups) % 2 == 0
+            if own or n == len(order) - 2:
+                g = 2 * flip(x, dx, n_x) + (k if own else 1 - k)
+                if not own:
+                    rows_there(g)
+                groups.append(g)
+                for early in seen:
+                    both(early, g * chunk, chunk)
     while chunks:
         rows_in(*chunks.pop(0))
 
     for dx in range(1, n_x):
-        other = flip(x, dx, n_x)
-        for t in range(chunk):
-            tile = (2 * other + (1 - k)) * chunk + t
-            arrived(e_buf.at[tile], e_send.at[0, 0], e_recv.at[tile])
         for kk in (k, 1 - k):
-            def far(b, carry):
-                both(b, (2 * other + kk) * chunk, chunk)
+            g = 2 * flip(x, dx, n_x) + kk
+            if small and 2 * (dx - 1) + (0 if kk is k else 1) < len(groups):
+                continue
+            if kk is not k:
+                rows_there(g)
+
+            def far(b, carry, g=g):
+                both(b, g * chunk, chunk)
                 return carry
 
             lax.fori_loop(0, n_b, far, 0)
@@ -254,7 +287,7 @@
     for peer in imp_peers:
         arrived(spend_recv.at[peer], spend_ssem.at[0], spend_rsem.at[peer])
         mine = mine + spend_recv[peer]
-    limit = limit_ref[...]
+    limit = limit_buf[...]
     new_ref[...] = price_buf[me_i] + 2.0 * (mine - limit) / (mine + limit)
     for copy in sends:
         copy.wait_send()
@@ -267,6 +300,7 @@
     n_b = n_imp
     n_z = n_imp // n_y
     n_x = n_camp // 2
+    slots = block_lists.shape[2]
     f32, bf16 = jnp.float32, jnp.bfloat16
     stored = n_b * n_t * BLOCK * LANES * 4 <= STORE_LIMIT
     dma = pltpu.SemaphoreType.DMA
@@ -277,7 +311,7 @@
             jax.ShapeDtypeStruct((1, LANES), f32),
             jax.ShapeDtypeStruct((n_t, LANES), f32),
         ),
-        in_specs=[anywhere, anywhere, anywhere, anywhere, vmem, vmem, vmem],
+        in_specs=[anywhere] * 7,
         out_specs=(vmem, vmem),
         scratch_shapes=[
             pltpu.VMEM((n_t, BLOCK, D), bf16),
@@ -294,7 +328,13 @@
             pltpu.VMEM((n_camp, 2, n_t, LANES), f32),
             pltpu.VMEM((n_b, 1, LANES), f32),
             pltpu.VMEM((n_b, 1, LANES), f32),
-            dma((4,)),
+            pltpu.VMEM((chunk * LANES,), bf16),
+            pltpu.VMEM((LANES,), bf16),
+            pltpu.VMEM((LANES, LANES), jnp.int32),
+            pltpu.VMEM((slots, n_t), jnp.int32),
+            pltpu.VMEM((1, n_t), jnp.int32),
+            pltpu.VMEM((1, LANES), f32),
+            dma((7,)),
             dma((n_x, chunk)),
             dma((n_x, chunk)),
             dma((n_t,)),
@@ -315,12 +355,12 @@
         ),
     )(
         imp_emb.reshape(chunk, BLOCK, D),
-        imp_cost.astype(f32).reshape(chunk, LANES),
+        imp_cost,
         camp_emb,
-        prices.astype(f32).reshape(1, LANES),
+        prices,
         spend_limits.reshape(1, LANES),
-        block_lists.reshape(n_t, -1),
-        block_counts,
+        block_lists.transpose(1, 2, 0).reshape(slots, n_t),
+        block_counts.T,
     )
     return new_prices.reshape(-1), logz.reshape(-1)
 

time: 38.6 us -> 30.9 us (0.80)
  Pallas kernels: 32.6 us -> 28.3 us
  local copies, waits for them, and re-layouts: 3.94 us -> 1.79 us
  other arithmetic: 1.1 us -> 0 us
    pallas_call x1, Pallas kernels: 32.6 us -> 28.3 us  [local(): pl.pallas_call(functools.partial(kernel, (n_imp, n_camp, n_y, chunk)), ou...]
    unnamed x13 -> x4, local copies, waits for them, and re-layouts: 3.28 us -> 1.79 us
    reshape x2 -> x0, other arithmetic: 1.1 us -> none  [the longest x1 0.59 us: local(): imp_cost.astype(f32).reshape(chunk, LANES)]
    reshape x1 -> x0, local copies, waits for them, and re-layouts: 0.67 us -> none  [local(): block_lists.reshape(n_t, -1)]
where the time goes in v2:
time: 30.9 us; the launch traced here: 30.7 us
  Pallas kernels  28.3 us (92%)
  local copies, waits for them, and re-layouts  1.79 us (6%)
  between operations  0.65 us (2%)
    pallas_call x1, Pallas kernels, local(): pl.pallas_call(functools.partial(kernel, (n_imp, n_camp, n_y, chunk)), ou...  28.3 us
    unnamed x4, local copies, waits for them, and re-layouts  1.79 us

profile of v2, /device:TPU:0, one launch (start us, length us, event | category | flops | bytes accessed | tf_op | source)
XLA Modules:
  0.0 30.7 jit_solution(4613884130526397983)
XLA Ops:
  0.6 28.3 %shard_map.86 = (f32[1,128]{1,0:T(1,128)}, f32[16,128]{1,0:T(8,128)}) custom-call(bf16[4,128,256]{2,1,0:T(8,128)(2,1)} %bitcast.8, bf16[512]{0:T(512)(128)(2,1)} %cost_ref.1, bf16[128,256]{1,0:T(8,128)(2,1)} %camp_ref.1, bf16[128]{0:T(256)(128)(2,1)} %price_ref.1, f32[1,128]{1,0:T(1,128)} %bitcast.11, s32[8,16]{1,0:T(8,128)} %bitcast.10, s32[1,16]{1,0:T(1,128)} %bitcast.12), custom_call_target="tpu_custom_call" | custom-call | tf_op jit(solution)/shard_map/pallas_call | solution.py:308
  28.9 0.0 copy-start
  28.9 1.2 %copy.11 = f32[128]{0:T(128)} copy(f32[128]{0:T(128)} %bitcast.13) | data formatting | bytes 1024
  30.1 0.0 copy-done
  30.1 0.6 %copy.12 = f32[2048]{0:T(1024)} copy(f32[2048]{0:T(1024)S(1)} %bitcast.9) | data formatting | bytes 16384
Async XLA Ops:
  28.9 1.2 %copy-start = (f32[16,128]{1,0:T(8,128)S(1)}, f32[16,128]{1,0:T(8,128)}, u32[]{:S(2)}) copy-start(f32[16,128]{1,0:T(8,128)} %get-tuple-element.5) | copy-start | bytes 24580

commit v3 on v2

--- a/solution.py
+++ b/solution.py
@@ -93,7 +93,7 @@
         live_buf[b] = jnp.broadcast_to(hit, (n_t, LANES))
         return carry
 
-    lax.fori_loop(0, n_b, mark, 0)
+    lax.fori_loop(0, n_b, mark, 0, unroll=n_b <= 8)
     price_buf[me_i] = price_raw[...].astype(jnp.float32).reshape(1, LANES)
     cost_buf[me_c] = cost_raw[...].astype(jnp.float32).reshape(chunk, LANES)
     pl.semaphore_wait(barrier, len(imp_peers) + len(camp_peers))
@@ -231,11 +231,11 @@
 
     top_here = lax.fori_loop(
         0, n_b, lambda b, top: jnp.maximum(top, block_top(b)),
-        jnp.full((n_t, LANES), -jnp.inf, jnp.float32),
+        jnp.full((n_t, LANES), -jnp.inf, jnp.float32), unroll=n_b <= 8,
     )
     total_here = lax.fori_loop(
         0, n_b, lambda b, total: total + s_buf[b] * jnp.exp(block_top(b) - top_here),
-        jnp.zeros((n_t, LANES), jnp.float32),
+        jnp.zeros((n_t, LANES), jnp.float32), unroll=n_b <= 8,
     )
     stat_send[0] = top_here
     stat_send[1] = total_here
@@ -260,7 +260,7 @@
         f_buf[b] = ratio * jnp.exp(block_top(b) - top)
         return carry
 
-    lax.fori_loop(0, n_b, factor, 0)
+    lax.fori_loop(0, n_b, factor, 0, unroll=n_b <= 8)
 
     def spend_of(b):
         def step(h, acc):
@@ -362,6 +362,20 @@
         block_lists.transpose(1, 2, 0).reshape(slots, n_t),
         block_counts.T,
     )
+
+    def hand(a_ref, b_ref, c_ref, d_ref):
+        c_ref[...] = a_ref[...]
+        d_ref[...] = b_ref[...]
+
+    new_prices, logz = pl.pallas_call(
+        hand,
+        out_shape=(
+            jax.ShapeDtypeStruct((1, LANES), f32),
+            jax.ShapeDtypeStruct((n_t, LANES), f32),
+        ),
+        in_specs=[vmem] * 2,
+        out_specs=(vmem, vmem),
+    )(new_prices, logz)
     return new_prices.reshape(-1), logz.reshape(-1)
 
 

time: 30.9 us -> 30.2 us (0.977)
  local copies, waits for them, and re-layouts: 1.79 us -> 0 us
  Pallas kernels: 28.3 us -> 29.4 us
    unnamed x4 -> x0, local copies, waits for them, and re-layouts: 1.79 us -> none
    pallas_call x0 -> x1, Pallas kernels: none -> 1.31 us  [local(): pl.pallas_call(hand, out_shape=(jax.ShapeDtypeStruct((1, LANES), f32), ja...]
where the time goes in v3:
time: 30.2 us; the launch traced here: 30 us
  Pallas kernels  29.4 us (97%)
  between operations  0.64 us (2%)
    pallas_call x1, Pallas kernels, local(): pl.pallas_call(functools.partial(kernel, (n_imp, n_camp, n_y, chunk)), ou...  28.1 us
    pallas_call x1, Pallas kernels, local(): pl.pallas_call(hand, out_shape=(jax.ShapeDtypeStruct((1, LANES), f32), ja...  1.31 us

profile of v3, /device:TPU:0, one launch (start us, length us, event | category | flops | bytes accessed | tf_op | source)
XLA Modules:
  0.0 30.0 jit_solution(13318857399663424521)
XLA Ops:
  0.6 28.1 %shard_map.86 = (f32[1,128]{1,0:T(1,128)}, f32[16,128]{1,0:T(8,128)}) custom-call(bf16[4,128,256]{2,1,0:T(8,128)(2,1)} %bitcast.8, bf16[512]{0:T(512)(128)(2,1)} %cost_ref.1, bf16[128,256]{1,0:T(8,128)(2,1)} %camp_ref.1, bf16[128]{0:T(256)(128)(2,1)} %price_ref.1, f32[1,128]{1,0:T(1,128)} %bitcast.10, s32[8,16]{1,0:T(8,128)} %bitcast.9, s32[1,16]{1,0:T(1,128)} %bitcast.11), custom_call_target="tpu_custom_call" | custom-call | tf_op jit(solution)/shard_map/pallas_call | solution.py:308
  28.7 1.3 %shard_map.87 = (f32[1,128]{1,0:T(1,128)}, f32[16,128]{1,0:T(8,128)}) custom-call(f32[1,128]{1,0:T(1,128)} %get-tuple-element.6.a_ref, f32[16,128]{1,0:T(8,128)} %get-tuple-element.7.b_ref), custom_call_target="tpu_custom_call" | custom-call | tf_op jit(solution)/shard_map/pallas_call | solution.py:370
